TPU v7x, 32 devices: a whole 2x2x4 slice. The times are simulated.
32 devices in a mesh: region: 4 (over y, x), block: 8 (over z, core).
Axes of the slice: x: 2, y: 2, z: 4, core: 2. Of those that a mesh axis runs over, the one named last changes fastest.
Arguments:
- obs: bfloat16 [512, 32, 128], P(('region', 'block')), may hold values from -6 to 6
- predict: bfloat16 [512, 2, 128, 128], P(('region', 'block')), may hold values from -0.375 to 0.375
- factor: bfloat16 [512, 128, 128], P(('region', 'block')), as said below
- tau: float32 [32], replicated, may hold values from 0.5 to 2
- nbr_dev: int32 [512, 1], P(('region', 'block')), may hold values from 0 to 7; in each aligned block of 16 rows (0 to 15, 16 to 31, ...) at most 4 rows name the same one
- nbr_slot: int32 [512, 2], P(('region', 'block')), may hold values from 0 to 15
- counts: int32 [32], P(('region', 'block')), may hold values from 8 to 16
Outputs:
- grad_obs: float32 [512, 32, 128], P(('region', 'block'))
- grad_tau: float32 [32], replicated
Inputs may be any that keep to these rules, and one draw needn't show every extreme that they name: `nbr_dev`: among the blocks of one device at most 4 name the same device. `nbr_slot`: column 0 is a slot on the in-region neighbour's device, column 1 a slot on the device of the previous region with the same index along block. `factor`: each block's matrix is the identity plus small entries.
All inputs are finite; a program needn't handle non-finite values.
Results may differ from a plain program's by a relative error of at most 0.0035.
Values may be sent and summed in bfloat16 or wider, within the bound.
A program may use at most 64 MiB of HBM per device.

v0:
```python
import jax
import jax.numpy as jnp
from jax import lax
from jax.sharding import PartitionSpec as P


def passed_along(value, axis, steps):
    count = lax.axis_size(axis)
    leading, last = (max(0, -steps), min(count, count - steps))
    return lax.ppermute(value, axis, [(source, source + steps) for source in range(leading, last)])


def shards(obs, predict, factor, tau, nbr_dev, nbr_slot, counts):
    nbd = obs.shape[0]
    chans = obs.shape[1]
    width = obs.shape[2]
    nblock = lax.axis_size("block")
    cap_size = max(2, 2 * nbd // nblock)
    total_slots = nblock * cap_size
    dest = nbr_dev[:, 0]
    slot_one = nbr_slot[:, 0]
    slot_two = nbr_slot[:, 1]
    onehot = (dest[:, None] == jnp.arange(nblock, dtype=jnp.int32)[None, :]).astype(jnp.int32)
    before = jnp.cumsum(onehot, axis=0) - onehot
    rank_in = jnp.sum(before * onehot, axis=1)
    flat = dest * cap_size + rank_in
    match = (flat[:, None] == jnp.arange(total_slots, dtype=jnp.int32)[None, :]).astype(jnp.int32)
    filled = jnp.sum(match, axis=0)
    req_flat = jnp.sum(match * slot_one[:, None], axis=0) + (1 - filled) * nbd
    request = req_flat.reshape(nblock, cap_size)
    region_all = lax.all_gather(obs, "block", axis=0, tiled=True)
    near = jnp.take(region_all, dest * nbd + slot_one, axis=0)
    previous = passed_along(obs, "region", 1)
    far = jnp.take(previous, slot_two, axis=0)
    p_zero = predict[:, 0]
    p_one = predict[:, 1]
    err = obs.astype(jnp.float32) - jnp.einsum(
        "bcj,bjk->bck", near, p_zero, preferred_element_type=jnp.float32
    )
    err = err - jnp.einsum("bcj,bjk->bck", far, p_one, preferred_element_type=jnp.float32)
    err = err.astype(jnp.bfloat16)
    white = jnp.einsum("bcj,bjk->bck", err, factor, preferred_element_type=jnp.float32)
    live = (jnp.arange(nbd, dtype=jnp.int32) < counts[0]).astype(jnp.float32)
    weighted = (live[:, None, None] * tau[None, :, None] * white).astype(jnp.bfloat16)
    adj = jnp.einsum("bck,bjk->bcj", weighted, factor, preferred_element_type=jnp.float32)
    adj16 = adj.astype(jnp.bfloat16)
    back_one = -jnp.einsum("bck,bjk->bcj", adj16, p_zero, preferred_element_type=jnp.float32)
    back_two = -jnp.einsum("bck,bjk->bcj", adj16, p_one, preferred_element_type=jnp.float32)
    placed = jnp.einsum(
        "bs,bcj->scj", match.astype(jnp.float32), back_one, precision=lax.Precision.HIGHEST
    )
    placed = placed.reshape(nblock, cap_size, chans, width)
    returned, owned_slots = (
        lax.all_to_all(placed, "block", split_axis=0, concat_axis=0, tiled=True),
        lax.all_to_all(request, "block", split_axis=0, concat_axis=0, tiled=True),
    )
    spread = (owned_slots.reshape(-1)[:, None] == jnp.arange(nbd, dtype=jnp.int32)[None, :]).astype(
        jnp.float32
    )
    add_one = jnp.einsum(
        "sb,scj->bcj",
        spread,
        returned.reshape(total_slots, chans, width),
        precision=lax.Precision.HIGHEST,
    )
    seam_hot = (slot_two[:, None] == jnp.arange(nbd, dtype=jnp.int32)[None, :]).astype(jnp.float32)
    seam_dense = jnp.einsum("bs,bcj->scj", seam_hot, back_two, precision=lax.Precision.HIGHEST)
    add_two = passed_along(seam_dense, "region", -1)
    grad_obs = adj + add_one + add_two
    squares = jnp.sum(live[:, None, None] * white * white, axis=(0, 2))
    live_count = jnp.sum(live)
    total_sq, total_live = lax.psum((squares, live_count), ("region", "block"))
    all_blocks = nbd * lax.axis_size("region") * nblock
    grad_tau = (0.5 * total_sq - 0.5 * width * total_live / tau) / (all_blocks * width)
    return (grad_obs, grad_tau)


def solution(mesh):
    in_specs = (
        P(("region", "block"), None, None),
        P(("region", "block"), None, None, None),
        P(("region", "block"), None, None),
        P(),
        P(("region", "block"), None),
        P(("region", "block"), None),
        P(("region", "block")),
    )
    out_specs = (P(("region", "block"), None, None), P())
    return jax.shard_map(shards, mesh=mesh, in_specs=in_specs, out_specs=out_specs, check_vma=False)
```

profile of v0, /device:TPU:0, one launch (start us, length us, event | category | flops | bytes accessed | tf_op | source)
XLA Modules:
  0.0 102.5 jit_solution(590737278167899570)
XLA Ops:
  7.2 0.7 all-gather.2.cloned.1.call-update
  7.9 0.2 copy-done.2
  8.1 4.8 %collective-permute-start = (bf16[16,32,128]{2,1,0:T(8,128)(2,1)S(1)}, bf16[16,32,128]{2,1,0:T(8,128)(2,1)S(1)}, u32[]{:S(2)}, u32[]{:S(2)}) collective-permute-start(bf16[16,32,128]{2,1,0:T(8,128)(2,1)S(1)} %copy-done.2), channel_id=1, source_target_pairs={{0,8},{8,16},{16,24},{1,9},{9,17},{17,25},{2,10},{10,18},{18,26},{... | collective-permute-start | bytes 393224 | tf_op jit(solution)/shard_map/ppermute | solution.py:10
  13.0 0.7 fusion.33
  13.8 0.8 select_reduce_fusion.1
  14.6 0.8 slice_bitcast_fusion.1
  15.5 0.7 add.50
  16.1 4.9 %all-to-all-start = ((s32[8,1,4]{2,1,0:T(1,128)}), s32[8,1,4]{2,1,0:T(1,128)S(1)}, u32[]{:S(2)}, u32[]{:S(2)}) async-start(s32[8,1,4]{2,1,0:T(1,128)} %bitcast.11), calls=%async_computation | async-start | bytes 8192 | tf_op jit(solution)/shard_map/all_to_all | solution.py:55
  21.7 0.8 and_bitcast_fusion.1
  22.4 0.7 broadcast_multiply_fusion
  23.2 0.6 gather_fusion.1
  23.8 10.7 %all-gather.2.cloned.1.call-done = bf16[128,32,128]{2,1,0:T(8,128)(2,1)} async-done(((bf16[16,32,128]{2,1,0:T(8,128)(2,1)}), bf16[128,32,128]{2,1,0:T(8,128)(2,1)}) %all-gather.2.cloned.1.call-update) | async-done | bytes 1048592 | tf_op jit(solution)/shard_map/all_gather | solution.py:31
  34.5 1.8 %gather_fusion = bf16[16,32,128]{2,1,0:T(8,128)(2,1)S(1)} fusion(bf16[128,32,128]{2,1,0:T(8,128)(2,1)} %all-gather.2.cloned.1.call-done, s32[1024]{0:T(1024)S(1)} %pad_clamp_fusion.1), kind=kCustom, calls=%fused_computation | custom fusion | bytes 262208 | tf_op jit(solution)/shard_map/jit(_take)/gather | solution.py:32
  36.3 1.4 %convolution_subtract_fusion.1 = f32[16,32,128]{2,1,0:T(8,128)S(1)} fusion(bf16[16,2,128,128]{3,2,1,0:T(8,128)(2,1)} %param.8, bf16[16,32,128]{2,1,0:T(8,128)(2,1)S(1)} %copy-done.2, bf16[16,32,128]{2,1,0:T(8,128)(2,1)S(1)} %gather_fusion, pred[16]{0:T(512)(128)(4,1)S(1)} %get-tuple-element.6), kind=kOutput, calls=%fused_computation.5 | convolution fusion | flops 16973824 | bytes 1048592 | tf_op jit(solution)/shard_map/bcj,bjk->bck/dot_general | solution.py:37
  37.7 0.6 fusion.12
  38.2 0.4 fusion.18
  38.6 0.4 convolution_negate_fusion.1
  39.0 0.7 fusion.16
  39.8 0.9 copy.17
  40.7 3.5 %all-to-all-start.1 = ((f32[8,4,32,128]{3,1,2,0:T(4,128)}), f32[8,4,32,128]{3,1,2,0:T(4,128)S(1)}, u32[]{:S(2)}, u32[]{:S(2)}) async-start(f32[8,4,32,128]{3,1,2,0:T(4,128)} %copy.17), calls=%async_computation.1 | async-start | bytes 1048576 | tf_op jit(solution)/shard_map/all_to_all | solution.py:54
  44.2 0.6 fusion.47
  44.8 0.5 broadcast.119
  45.3 0.7 reduce.3
  46.0 0.4 convolution_negate_fusion
  46.4 0.4 fusion.13
  46.9 1.3 %collective-permute-start.1 = (f32[16,32,128]{2,1,0:T(8,128)S(1)}, f32[16,32,128]{2,1,0:T(8,128)S(1)}, u32[]{:S(2)}, u32[]{:S(2)}) collective-permute-start(f32[16,32,128]{2,1,0:T(8,128)S(1)} %copy.21), channel_id=1, source_target_pairs={{8,0},{16,8},{24,16},{9,1},{17,9},{25,17},{10,2},{18,10},{26,18},{... | collective-permute-start | bytes 786440 | tf_op jit(solution)/shard_map/ppermute | solution.py:10
  48.2 44.3 %all-reduce = (f32[32]{0:T(128)S(1)}, f32[]{:T(128)}) all-reduce(f32[32]{0:T(128)S(1)} %get-tuple-element.12, f32[]{:T(128)} %fusion.47), channel_id=1, replica_groups=mesh['region'=4,'block'=8] {'region','block'}, use_global_device_ids=true, to_apply=%region_5.6 | all-reduce | flops 33 | bytes 264 | tf_op jit(solution)/shard_map/psum | solution.py:72
  93.2 0.6 copy-done.3
  93.8 0.5 fusion.43
  94.3 0.1 copy.18
  94.5 0.3 fusion.35
  94.8 0.9 fusion.15
  (19 shorter events, 0.4 us)
Async XLA Ops:
  7.2 30.5 %copy-start = (bf16[16,128,128]{2,1,0:T(8,128)(2,1)S(1)}, bf16[16,128,128]{2,1,0:T(8,128)(2,1)}, u32[]{:S(2)}) copy-start(bf16[16,128,128]{2,1,0:T(8,128)(2,1)} %param.9) | copy-start | bytes 1572868
  7.2 1.0 copy-start.2
  7.2 30.5 %copy-start.1 = (bf16[16,2,128,128]{3,2,1,0:T(8,128)(2,1)S(1)}, bf16[16,2,128,128]{3,2,1,0:T(8,128)(2,1)}, u32[]{:S(2)}) copy-start(bf16[16,2,128,128]{3,2,1,0:T(8,128)(2,1)} %param.8) | copy-start | bytes 3145732
  7.2 27.3 %all-gather.2.cloned.1.call-start = ((), (), s32[]{:S(2)}) async-start(), calls=%async_computation.2 | async-start | bytes 1179648 | tf_op jit(solution)/shard_map/all_gather | solution.py:31
  8.1 15.0 %collective-permute-start = (bf16[16,32,128]{2,1,0:T(8,128)(2,1)S(1)}, bf16[16,32,128]{2,1,0:T(8,128)(2,1)S(1)}, u32[]{:S(2)}, u32[]{:S(2)}) collective-permute-start(bf16[16,32,128]{2,1,0:T(8,128)(2,1)S(1)} %copy-done.2), channel_id=1, source_target_pairs={{0,8},{8,16},{16,24},{1,9},{9,17},{17,25},{2,10},{10,18},{18,26},{... | collective-permute-start | bytes 393224 | tf_op jit(solution)/shard_map/ppermute | solution.py:10
  16.1 24.5 %all-to-all-start = ((s32[8,1,4]{2,1,0:T(1,128)}), s32[8,1,4]{2,1,0:T(1,128)S(1)}, u32[]{:S(2)}, u32[]{:S(2)}) async-start(s32[8,1,4]{2,1,0:T(1,128)} %bitcast.11), calls=%async_computation | async-start | bytes 8192 | tf_op jit(solution)/shard_map/all_to_all | solution.py:55
  40.7 53.7 %all-to-all-start.1 = ((f32[8,4,32,128]{3,1,2,0:T(4,128)}), f32[8,4,32,128]{3,1,2,0:T(4,128)S(1)}, u32[]{:S(2)}, u32[]{:S(2)}) async-start(f32[8,4,32,128]{3,1,2,0:T(4,128)} %copy.17), calls=%async_computation.1 | async-start | bytes 1048576 | tf_op jit(solution)/shard_map/all_to_all | solution.py:54
  46.9 47.9 %collective-permute-start.1 = (f32[16,32,128]{2,1,0:T(8,128)S(1)}, f32[16,32,128]{2,1,0:T(8,128)S(1)}, u32[]{:S(2)}, u32[]{:S(2)}) collective-permute-start(f32[16,32,128]{2,1,0:T(8,128)S(1)} %copy.21), channel_id=1, source_target_pairs={{8,0},{16,8},{24,16},{9,1},{17,9},{25,17},{10,2},{18,10},{26,18},{... | collective-permute-start | bytes 786440 | tf_op jit(solution)/shard_map/ppermute | solution.py:10
  93.1 0.7 copy-start.3
Sparse Core Ops, SparseCore 0:
  9.6 24.7 all-gather.1
where the time goes:
time: 103 us
  blocking collectives  44.3 us (43%)
  between operations  15.5 us (15%)
  starting transfers between devices  14.5 us (14%)
  waiting for transfers between devices  11.4 us (11%)
  other arithmetic  6.61 us (6%)
  local copies, waits for them, and re-layouts  5.62 us (5%)
  matrix products  4.57 us (4%)
    psum x1, blocking collectives, shards(): total_sq, total_live = lax.psum((squares, live_count), ('region', 'block'))  44.3 us
    all_gather x1, waiting for transfers between devices, shards(): region_all = lax.all_gather(obs, 'block', axis=0, tiled=True)  10.7 us
    ppermute x2, starting transfers between devices, passed_along(): lax.ppermute(value, axis, [(source, source + steps) for source in range(l...  6.13 us
    all_to_all x1, starting transfers between devices, shards(): lax.all_to_all(request, 'block', split_axis=0, concat_axis=0, tiled=True)  4.88 us
    all_to_all x1, starting transfers between devices, shards(): lax.all_to_all(placed, 'block', split_axis=0, concat_axis=0, tiled=True)  3.49 us
  transfers between devices with their start and end apart: 5, of which 1 were waited for; matrix products, arithmetic and copies ran while one was open for 15% of the time, Pallas kernels for 0%

commit v1 on v0

--- a/solution.py
+++ b/solution.py
@@ -69,7 +69,13 @@
     grad_obs = adj + add_one + add_two
     squares = jnp.sum(live[:, None, None] * white * white, axis=(0, 2))
     live_count = jnp.sum(live)
-    total_sq, total_live = lax.psum((squares, live_count), ("region", "block"))
+
+    def bring_figure_by_axis(field_in, ax_name, link_axis):
+        for at in (ax_name, link_axis):
+            field_in = jax.lax.psum(field_in, at)
+        return field_in
+
+    total_sq, total_live = bring_figure_by_axis((squares, live_count), "block", "region")
     all_blocks = nbd * lax.axis_size("region") * nblock
     grad_tau = (0.5 * total_sq - 0.5 * width * total_live / tau) / (all_blocks * width)
     return (grad_obs, grad_tau)

time: 103 us -> 87.9 us (0.85)
  blocking collectives: 44.3 us -> 29.2 us
    psum x1 -> x2, blocking collectives: 44.3 us -> 29.2 us  [bring_figure_by_axis(): field_in = jax.lax.psum(field_in, at)]
  transfers between devices with their start and end apart: 5 -> 5, of which waited for: 1 -> 1; matrix products, arithmetic and copies ran while one was open for 15% -> 17% of each run, Pallas kernels for 0% -> 0%
where the time goes in v1:
time: 87.9 us; the launch traced here: 87.4 us
  blocking collectives  29.2 us (33%)
  between operations  15.5 us (18%)
  starting transfers between devices  14.5 us (16%)
  waiting for transfers between devices  11.4 us (13%)
  other arithmetic  6.61 us (8%)
  local copies, waits for them, and re-layouts  5.62 us (6%)
  matrix products  4.57 us (5%)
    psum x2, blocking collectives, bring_figure_by_axis(): field_in = jax.lax.psum(field_in, at)  29.2 us
    all_gather x1, waiting for transfers between devices, shards(): region_all = lax.all_gather(obs, 'block', axis=0, tiled=True)  10.7 us
    ppermute x2, starting transfers between devices, passed_along(): lax.ppermute(value, axis, [(source, source + steps) for source in range(l...  6.13 us
    all_to_all x1, starting transfers between devices, shards(): lax.all_to_all(request, 'block', split_axis=0, concat_axis=0, tiled=True)  4.88 us
    all_to_all x1, starting transfers between devices, shards(): lax.all_to_all(placed, 'block', split_axis=0, concat_axis=0, tiled=True)  3.49 us
    gather x1, local copies, waits for them, and re-layouts, shards(): near = jnp.take(region_all, dest * nbd + slot_one, axis=0)  1.8 us
  transfers between devices with their start and end apart: 5, of which 1 were waited for; matrix products, arithmetic and copies ran while one was open for 17% of the time, Pallas kernels for 0%

profile of v1, /device:TPU:0, one launch (start us, length us, event | category | flops | bytes accessed | tf_op | source)
XLA Modules:
  0.0 87.4 jit_solution(10569275526177013040)
XLA Ops:
  7.2 0.7 all-gather.2.cloned.1.call-update
  7.9 0.2 copy-done.2
  8.1 4.8 %collective-permute-start = (bf16[16,32,128]{2,1,0:T(8,128)(2,1)S(1)}, bf16[16,32,128]{2,1,0:T(8,128)(2,1)S(1)}, u32[]{:S(2)}, u32[]{:S(2)}) collective-permute-start(bf16[16,32,128]{2,1,0:T(8,128)(2,1)S(1)} %copy-done.2), channel_id=1, source_target_pairs={{0,8},{8,16},{16,24},{1,9},{9,17},{17,25},{2,10},{10,18},{18,26},{... | collective-permute-start | bytes 393224 | tf_op jit(solution)/shard_map/ppermute | solution.py:10
  13.0 0.7 fusion.33
  13.8 0.8 select_reduce_fusion.1
  14.6 0.8 slice_bitcast_fusion.1
  15.5 0.7 add.54
  16.1 4.9 %all-to-all-start = ((s32[8,1,4]{2,1,0:T(1,128)}), s32[8,1,4]{2,1,0:T(1,128)S(1)}, u32[]{:S(2)}, u32[]{:S(2)}) async-start(s32[8,1,4]{2,1,0:T(1,128)} %bitcast.11), calls=%async_computation | async-start | bytes 8192 | tf_op jit(solution)/shard_map/all_to_all | solution.py:55
  21.7 0.8 and_bitcast_fusion.1
  22.4 0.7 broadcast_multiply_fusion
  23.2 0.6 gather_fusion.1
  23.8 10.7 %all-gather.2.cloned.1.call-done = bf16[128,32,128]{2,1,0:T(8,128)(2,1)} async-done(((bf16[16,32,128]{2,1,0:T(8,128)(2,1)}), bf16[128,32,128]{2,1,0:T(8,128)(2,1)}) %all-gather.2.cloned.1.call-update) | async-done | bytes 1048592 | tf_op jit(solution)/shard_map/all_gather | solution.py:31
  34.5 1.8 %gather_fusion = bf16[16,32,128]{2,1,0:T(8,128)(2,1)S(1)} fusion(bf16[128,32,128]{2,1,0:T(8,128)(2,1)} %all-gather.2.cloned.1.call-done, s32[1024]{0:T(1024)S(1)} %pad_clamp_fusion.1), kind=kCustom, calls=%fused_computation | custom fusion | bytes 262208 | tf_op jit(solution)/shard_map/jit(_take)/gather | solution.py:32
  36.3 1.4 %convolution_subtract_fusion.1 = f32[16,32,128]{2,1,0:T(8,128)S(1)} fusion(bf16[16,2,128,128]{3,2,1,0:T(8,128)(2,1)} %param.8, bf16[16,32,128]{2,1,0:T(8,128)(2,1)S(1)} %copy-done.2, bf16[16,32,128]{2,1,0:T(8,128)(2,1)S(1)} %gather_fusion, pred[16]{0:T(512)(128)(4,1)S(1)} %get-tuple-element.8), kind=kOutput, calls=%fused_computation.5 | convolution fusion | flops 16973824 | bytes 1048592 | tf_op jit(solution)/shard_map/bcj,bjk->bck/dot_general | solution.py:37
  37.7 0.6 fusion.12
  38.2 0.4 fusion.18
  38.6 0.4 convolution_negate_fusion.1
  39.0 0.7 fusion.16
  39.8 0.9 %copy.17 = f32[8,4,32,128]{3,1,2,0:T(4,128)} copy(f32[8,4,32,128]{3,1,0,2:T(4,128)S(1)} %bitcast.53) | data formatting | bytes 1048576 | tf_op jit(solution)/shard_map/reshape | solution.py:52
  40.7 3.5 %all-to-all-start.1 = ((f32[8,4,32,128]{3,1,2,0:T(4,128)}), f32[8,4,32,128]{3,1,2,0:T(4,128)S(1)}, u32[]{:S(2)}, u32[]{:S(2)}) async-start(f32[8,4,32,128]{3,1,2,0:T(4,128)} %copy.17), calls=%async_computation.1 | async-start | bytes 1048576 | tf_op jit(solution)/shard_map/all_to_all | solution.py:54
  44.2 0.6 fusion.47
  44.8 0.5 broadcast.119
  45.3 0.7 reduce.3
  46.0 0.4 convolution_negate_fusion
  46.4 0.4 fusion.13
  46.9 1.3 %collective-permute-start.1 = (f32[16,32,128]{2,1,0:T(8,128)S(1)}, f32[16,32,128]{2,1,0:T(8,128)S(1)}, u32[]{:S(2)}, u32[]{:S(2)}) collective-permute-start(f32[16,32,128]{2,1,0:T(8,128)S(1)} %copy.21), channel_id=1, source_target_pairs={{8,0},{16,8},{24,16},{9,1},{17,9},{25,17},{10,2},{18,10},{26,18},{... | collective-permute-start | bytes 786440 | tf_op jit(solution)/shard_map/ppermute | solution.py:10
  48.2 18.0 %all-reduce = (f32[32]{0:T(128)S(1)}, f32[]{:T(128)}) all-reduce(f32[32]{0:T(128)S(1)} %get-tuple-element.14, f32[]{:T(128)} %fusion.47), channel_id=1, replica_groups=mesh['region'=4,'block'=8] {'block'}, use_global_device_ids=true, to_apply=%region_5.6 | all-reduce | flops 33 | bytes 264 | tf_op jit(solution)/shard_map/psum | solution.py:75
  66.2 11.2 %all-reduce.1 = (f32[32]{0:T(128)S(1)}, f32[]{:T(128)}) all-reduce(f32[32]{0:T(128)S(1)} %get-tuple-element.4, f32[]{:T(128)} %get-tuple-element.5), channel_id=1, replica_groups=mesh['region'=4,'block'=8] {'region'}, use_global_device_ids=true, to_apply=%region_6.7 | all-reduce | flops 33 | bytes 264 | tf_op jit(solution)/shard_map/psum | solution.py:75
  78.1 0.6 copy-done.3
  78.7 0.5 fusion.43
  79.4 0.3 fusion.35
  79.7 0.9 fusion.15
  (20 shorter events, 0.5 us)
Async XLA Ops:
  7.2 30.5 %copy-start = (bf16[16,128,128]{2,1,0:T(8,128)(2,1)S(1)}, bf16[16,128,128]{2,1,0:T(8,128)(2,1)}, u32[]{:S(2)}) copy-start(bf16[16,128,128]{2,1,0:T(8,128)(2,1)} %param.9) | copy-start | bytes 1572868
  7.2 1.0 %copy-start.2 = (bf16[16,32,128]{2,1,0:T(8,128)(2,1)S(1)}, bf16[16,32,128]{2,1,0:T(8,128)(2,1)}, u32[]{:S(2)}) copy-start(bf16[16,32,128]{2,1,0:T(8,128)(2,1)} %param.7) | copy-start | bytes 393220
  7.2 30.5 %copy-start.1 = (bf16[16,2,128,128]{3,2,1,0:T(8,128)(2,1)S(1)}, bf16[16,2,128,128]{3,2,1,0:T(8,128)(2,1)}, u32[]{:S(2)}) copy-start(bf16[16,2,128,128]{3,2,1,0:T(8,128)(2,1)} %param.8) | copy-start | bytes 3145732
  7.2 27.3 %all-gather.2.cloned.1.call-start = ((), (), s32[]{:S(2)}) async-start(), calls=%async_computation.2 | async-start | bytes 1179648 | tf_op jit(solution)/shard_map/all_gather | solution.py:31
  8.1 15.0 %collective-permute-start = (bf16[16,32,128]{2,1,0:T(8,128)(2,1)S(1)}, bf16[16,32,128]{2,1,0:T(8,128)(2,1)S(1)}, u32[]{:S(2)}, u32[]{:S(2)}) collective-permute-start(bf16[16,32,128]{2,1,0:T(8,128)(2,1)S(1)} %copy-done.2), channel_id=1, source_target_pairs={{0,8},{8,16},{16,24},{1,9},{9,17},{17,25},{2,10},{10,18},{18,26},{... | collective-permute-start | bytes 393224 | tf_op jit(solution)/shard_map/ppermute | solution.py:10
  16.1 24.5 %all-to-all-start = ((s32[8,1,4]{2,1,0:T(1,128)}), s32[8,1,4]{2,1,0:T(1,128)S(1)}, u32[]{:S(2)}, u32[]{:S(2)}) async-start(s32[8,1,4]{2,1,0:T(1,128)} %bitcast.11), calls=%async_computation | async-start | bytes 8192 | tf_op jit(solution)/shard_map/all_to_all | solution.py:55
  40.7 38.6 %all-to-all-start.1 = ((f32[8,4,32,128]{3,1,2,0:T(4,128)}), f32[8,4,32,128]{3,1,2,0:T(4,128)S(1)}, u32[]{:S(2)}, u32[]{:S(2)}) async-start(f32[8,4,32,128]{3,1,2,0:T(4,128)} %copy.17), calls=%async_computation.1 | async-start | bytes 1048576 | tf_op jit(solution)/shard_map/all_to_all | solution.py:54
  46.9 32.8 %collective-permute-start.1 = (f32[16,32,128]{2,1,0:T(8,128)S(1)}, f32[16,32,128]{2,1,0:T(8,128)S(1)}, u32[]{:S(2)}, u32[]{:S(2)}) collective-permute-start(f32[16,32,128]{2,1,0:T(8,128)S(1)} %copy.21), channel_id=1, source_target_pairs={{8,0},{16,8},{24,16},{9,1},{17,9},{25,17},{10,2},{18,10},{26,18},{... | collective-permute-start | bytes 786440 | tf_op jit(solution)/shard_map/ppermute | solution.py:10
  78.1 0.7 copy-start.3
Sparse Core Ops, SparseCore 0:
  9.6 24.7 all-gather.1
